TPU v7x, 32 devices: a whole 2x2x4 slice. The times are simulated.
32 devices in a mesh: dom: 4 (over y, x), freq: 8 (over z, core).
Axes of the slice: x: 2, y: 2, z: 4, core: 2. Of those that a mesh axis runs over, the one named last changes fastest.
Arguments:
- voltages: float32 [512, 8192], P('freq', 'dom'), may hold values from -5 to 5
- sources: float32 [512, 8192], P('freq', 'dom'), may hold values from -20 to 20
- terminals: int32 [2, 16384], P(None, 'dom'), may hold values from 0 to 2559, as said below
- elem_current: float32 [2, 16384], P(None, 'dom'), may hold values from 0.2 to 2
- elem_charge: float32 [2, 16384], P(None, 'dom'), may hold values from 0.1 to 1
- jacobi: float32 [256, 2, 2, 8192], P('freq', None, None, 'dom'), may hold values from -1.2 to 2
Outputs:
- residual: float32 [512, 8192], P('freq', 'dom')
- newton_step: float32 [512, 8192], P('freq', 'dom')
- residual_norm: float32 [], replicated
Inputs may be any that keep to these rules, and one draw needn't show every extreme that they name: `terminals`: A terminal value below 2048 is a node of the element's own partition; a value v of 2048 or more is node (v - 2048) % 128 of partition (v - 2048) // 128, one of that partition's first 128 nodes.
All inputs are finite; a program needn't handle non-finite values.
Results may differ from a plain program's by a relative error of at most 0.0003.
Values sent between devices are 32-bit elements; how exact they have to be, the bound alone decides.
A program may use at most 64 MiB of HBM per device.

v0:
```python
import math
import jax
import jax.numpy as jnp
from jax import lax
from jax.sharding import PartitionSpec as P

S = 512
trust_radius = 2.0


def transform_table(samples):
    row_index = jnp.arange(samples, dtype=jnp.int32)
    harmonic = row_index // 2
    is_sine = row_index % 2 == 1
    column = jnp.arange(samples, dtype=jnp.int32)
    order = jnp.where(harmonic == 0, jnp.where(is_sine, samples // 2, 0), harmonic)
    phase = (order[:, None] * column[None, :] % samples).astype(jnp.float32) * (
        2.0 * math.pi / samples
    )
    use_sine = is_sine & (harmonic > 0)
    values = jnp.where(use_sine[:, None], jnp.sin(phase), jnp.cos(phase))
    weight = jnp.where(harmonic == 0, math.sqrt(1.0 / samples), math.sqrt(2.0 / samples)).astype(
        jnp.float32
    )
    forward = values * weight[:, None]
    pairs = forward.reshape(samples // 2, 2, samples)
    rate = 2.0 / samples * jnp.arange(samples // 2, dtype=jnp.float32)
    derived = jnp.stack([pairs[:, 1], -pairs[:, 0]], axis=1) * rate[:, None, None]
    return jnp.concatenate([forward, derived.reshape(samples, samples)], axis=1)


def incidence_sum(flows, terminals, column_count):
    flow_rows = flows.shape[0]
    elem_count = flows.shape[1]
    block_size = math.gcd(elem_count, 512)
    block_count = elem_count // block_size
    flow_blocks = flows.reshape(flow_rows, block_count, block_size).transpose(1, 0, 2)
    term_blocks = terminals.reshape(2, block_count, block_size).transpose(1, 0, 2)
    columns = jnp.arange(column_count, dtype=jnp.int32)

    def accumulate(total, pieces):
        flow_piece, term_piece = pieces
        plus = (term_piece[0][:, None] == columns[None, :]).astype(jnp.float32)
        minus = (term_piece[1][:, None] == columns[None, :]).astype(jnp.float32)
        signed = plus - minus
        total = total + jnp.dot(
            flow_piece, signed, precision=lax.Precision.HIGHEST, preferred_element_type=jnp.float32
        )
        return (total, None)

    start = jnp.zeros((flow_rows, column_count), jnp.float32)
    total, unused = lax.scan(accumulate, start, (flow_blocks, term_blocks))
    return total


def body(voltages, sources, terminals, elem_current, elem_charge, jacobi):
    sample_rows, node_count = voltages.shape
    freq_count = lax.axis_size("freq")
    border_count = node_count // 16
    border = lax.all_gather(voltages[:, :border_count], "dom", axis=1, tiled=True)
    extended = jnp.concatenate([voltages, border], axis=1)
    across = extended[:, terminals[0]] - extended[:, terminals[1]]
    current = elem_current[0][None, :] * across + elem_current[1][None, :] * jnp.tanh(2.0 * across)
    charge = elem_charge[0][None, :] * across + elem_charge[1][None, :] * jnp.tanh(across)
    flows = jnp.concatenate([current, charge], axis=0)
    totals = incidence_sum(flows, terminals, extended.shape[1]).reshape(
        2, sample_rows, extended.shape[1]
    )
    incoming = lax.psum_scatter(totals[:, :, node_count:], "dom", scatter_dimension=2, tiled=True)
    owned = totals[:, :, :node_count]
    owned = jnp.concatenate(
        [owned[:, :, :border_count] + incoming, owned[:, :, border_count:]], axis=2
    )
    table = transform_table(S)
    node_block = node_count // freq_count
    grouped = owned.reshape(2, sample_rows, freq_count, node_block)
    block = lax.all_to_all(grouped, "freq", split_axis=2, concat_axis=1, tiled=True)
    flat = block.reshape(2 * S, block.shape[3])
    spectra = jnp.dot(
        table, flat, precision=lax.Precision.HIGHEST, preferred_element_type=jnp.float32
    )
    transformed = lax.all_to_all(spectra, "freq", split_axis=0, concat_axis=1, tiled=True)
    residual = transformed - sources
    pairs = residual.reshape(sample_rows // 2, 2, node_count)
    raw = -(jacobi[:, :, 0, :] * pairs[:, 0:1, :] + jacobi[:, :, 1, :] * pairs[:, 1:2, :])
    raw = raw.reshape(sample_rows, node_count)
    step_squares, residual_squares = lax.psum(
        (jnp.sum(raw * raw), jnp.sum(residual * residual)), ("dom", "freq")
    )
    entry_count = S * node_count * lax.axis_size("dom")
    spread = jnp.sqrt(step_squares / entry_count + 1e-06)
    newton_step = raw * jnp.minimum(1.0, trust_radius / spread)
    residual_norm = jnp.sqrt(residual_squares)
    return (residual, newton_step, residual_norm)


def solution(mesh):
    placed = (
        P("freq", "dom"),
        P("freq", "dom"),
        P(None, "dom"),
        P(None, "dom"),
        P(None, "dom"),
        P("freq", None, None, "dom"),
    )
    return jax.shard_map(
        body,
        mesh=mesh,
        in_specs=placed,
        out_specs=(P("freq", "dom"), P("freq", "dom"), P()),
        check_vma=False,
    )
```

profile of v0, /device:TPU:12, one launch (start us, length us, event | category | flops | bytes accessed | tf_op | source)
XLA Modules:
  0.0 226.3 jit_solution(1652507804169828235)
XLA Ops:
  7.2 1.4 copy.26
  8.6 9.0 %all_gather.3 = f32[64,512]{0,1:T(8,128)S(1)} all-gather(f32[64,128]{0,1:T(8,128)S(1)} %slice.85), channel_id=1, replica_groups=mesh['dom'=4,'freq'=8] {'dom'}, dimensions={1}, use_global_device_ids=true | all-gather | bytes 163840 | tf_op jit(solution)/shard_map/all_gather | solution.py:60
  17.8 14.1 %gather_fusion = f32[4096,64]{1,0:T(8,128)} fusion(f32[64,2560]{0,1:T(8,128)S(1)} %pad_maximum_fusion, s32[4096]{0:T(1024)S(1)} %broadcast_clamp_fusion.1), kind=kCustom, calls=%fused_computation | custom fusion | bytes 2113536 | tf_op jit(solution)/shard_map/gather | solution.py:62
  31.9 14.1 %gather_fusion.1 = f32[4096,64]{1,0:T(8,128)} fusion(f32[64,2560]{0,1:T(8,128)S(1)} %pad_maximum_fusion, s32[4096]{0:T(1024)S(1)} %broadcast_clamp_fusion), kind=kCustom, calls=%fused_computation.1 | custom fusion | bytes 2113536 | tf_op jit(solution)/shard_map/gather | solution.py:62
  45.9 2.4 %sub.30 = f32[4096,64]{1,0:T(8,128)S(1)} subtract(f32[4096,64]{1,0:T(8,128)} %gather_fusion, f32[4096,64]{1,0:T(8,128)} %gather_fusion.1) | non-fusion elementwise | flops 262144 | bytes 3145728 | tf_op jit(solution)/shard_map/sub | solution.py:62
  48.4 0.6 copy.27
  49.0 0.1 copy-done.5
  49.2 0.2 slice_reduce_fusion.3
  49.4 0.3 multiply_add_fusion.1
  49.7 0.2 maximum_bitcast_fusion
  49.9 1.1 copy-done.1
  51.0 35.5 %while.12 = (s32[]{:T(128)}, f32[128,2560]{1,0:T(8,128)S(1)}, f32[8,128,512]{2,1,0:T(8,128)S(1)}, s32[8,2,512]{2,1,0:T(2,128)S(1)}, s32[]{:T(128)}, /*index=5*/s32[]{:T(128)}, s32[]{}) while((s32[]{:T(128)}, f32[128,2560]{1,0:T(8,128)S(1)}, f32[8,128,512]{2,1,0:T(8,128)S(1)}, s32[8,2,512]{2,1,0:T(2,128)S(1)}, ...), condition=%wide.region_1.2_spmd.clone.clone, body=%wide.region_0.1_spmd.clone.clone.sunk | while | flops 2020474880 | bytes 2895983 | solution.py:52
  51.0 4.4 %fusion.52 = f32[128,2560]{1,0:T(8,128)S(1)} fusion(s32[512]{0:T(512)S(1)} %bitcast.65, s32[512]{0:T(512)S(1)} %bitcast.64, f32[128,2560]{1,0:T(8,128)S(1)} %get-tuple-element.133, pred[]{:T(512)S(6)} %compare.14, f32[8,128,512]{2,1,0:T(8,128)S(1)} %get-tuple-element.141, s32[]{:T(128)} %get-tuple-element.132), kind=kOutput, calls=%fused_computation.9.clone.1 | convolution fusion | flops 2020474880 | bytes 2887685 | tf_op jit(solution)/shard_map/while/body/eval_jaxpr/dot_general | solution.py:46
  55.5 4.4 %fusion.52 = f32[128,2560]{1,0:T(8,128)S(1)} fusion(s32[512]{0:T(512)S(1)} %bitcast.65, s32[512]{0:T(512)S(1)} %bitcast.64, f32[128,2560]{1,0:T(8,128)S(1)} %get-tuple-element.133, pred[]{:T(512)S(6)} %compare.14, f32[8,128,512]{2,1,0:T(8,128)S(1)} %get-tuple-element.141, s32[]{:T(128)} %get-tuple-element.132), kind=kOutput, calls=%fused_computation.9.clone.1 | convolution fusion | flops 2020474880 | bytes 2887685 | tf_op jit(solution)/shard_map/while/body/eval_jaxpr/dot_general | solution.py:46
  59.9 4.4 %fusion.52 = f32[128,2560]{1,0:T(8,128)S(1)} fusion(s32[512]{0:T(512)S(1)} %bitcast.65, s32[512]{0:T(512)S(1)} %bitcast.64, f32[128,2560]{1,0:T(8,128)S(1)} %get-tuple-element.133, pred[]{:T(512)S(6)} %compare.14, f32[8,128,512]{2,1,0:T(8,128)S(1)} %get-tuple-element.141, s32[]{:T(128)} %get-tuple-element.132), kind=kOutput, calls=%fused_computation.9.clone.1 | convolution fusion | flops 2020474880 | bytes 2887685 | tf_op jit(solution)/shard_map/while/body/eval_jaxpr/dot_general | solution.py:46
  64.4 4.4 %fusion.52 = f32[128,2560]{1,0:T(8,128)S(1)} fusion(s32[512]{0:T(512)S(1)} %bitcast.65, s32[512]{0:T(512)S(1)} %bitcast.64, f32[128,2560]{1,0:T(8,128)S(1)} %get-tuple-element.133, pred[]{:T(512)S(6)} %compare.14, f32[8,128,512]{2,1,0:T(8,128)S(1)} %get-tuple-element.141, s32[]{:T(128)} %get-tuple-element.132), kind=kOutput, calls=%fused_computation.9.clone.1 | convolution fusion | flops 2020474880 | bytes 2887685 | tf_op jit(solution)/shard_map/while/body/eval_jaxpr/dot_general | solution.py:46
  68.8 4.4 %fusion.52 = f32[128,2560]{1,0:T(8,128)S(1)} fusion(s32[512]{0:T(512)S(1)} %bitcast.65, s32[512]{0:T(512)S(1)} %bitcast.64, f32[128,2560]{1,0:T(8,128)S(1)} %get-tuple-element.133, pred[]{:T(512)S(6)} %compare.14, f32[8,128,512]{2,1,0:T(8,128)S(1)} %get-tuple-element.141, s32[]{:T(128)} %get-tuple-element.132), kind=kOutput, calls=%fused_computation.9.clone.1 | convolution fusion | flops 2020474880 | bytes 2887685 | tf_op jit(solution)/shard_map/while/body/eval_jaxpr/dot_general | solution.py:46
  73.2 4.4 %fusion.52 = f32[128,2560]{1,0:T(8,128)S(1)} fusion(s32[512]{0:T(512)S(1)} %bitcast.65, s32[512]{0:T(512)S(1)} %bitcast.64, f32[128,2560]{1,0:T(8,128)S(1)} %get-tuple-element.133, pred[]{:T(512)S(6)} %compare.14, f32[8,128,512]{2,1,0:T(8,128)S(1)} %get-tuple-element.141, s32[]{:T(128)} %get-tuple-element.132), kind=kOutput, calls=%fused_computation.9.clone.1 | convolution fusion | flops 2020474880 | bytes 2887685 | tf_op jit(solution)/shard_map/while/body/eval_jaxpr/dot_general | solution.py:46
  77.7 4.4 %fusion.52 = f32[128,2560]{1,0:T(8,128)S(1)} fusion(s32[512]{0:T(512)S(1)} %bitcast.65, s32[512]{0:T(512)S(1)} %bitcast.64, f32[128,2560]{1,0:T(8,128)S(1)} %get-tuple-element.133, pred[]{:T(512)S(6)} %compare.14, f32[8,128,512]{2,1,0:T(8,128)S(1)} %get-tuple-element.141, s32[]{:T(128)} %get-tuple-element.132), kind=kOutput, calls=%fused_computation.9.clone.1 | convolution fusion | flops 2020474880 | bytes 2887685 | tf_op jit(solution)/shard_map/while/body/eval_jaxpr/dot_general | solution.py:46
  82.1 4.4 %fusion.52 = f32[128,2560]{1,0:T(8,128)S(1)} fusion(s32[512]{0:T(512)S(1)} %bitcast.65, s32[512]{0:T(512)S(1)} %bitcast.64, f32[128,2560]{1,0:T(8,128)S(1)} %get-tuple-element.133, pred[]{:T(512)S(6)} %compare.14, f32[8,128,512]{2,1,0:T(8,128)S(1)} %get-tuple-element.141, s32[]{:T(128)} %get-tuple-element.132), kind=kOutput, calls=%fused_computation.9.clone.1 | convolution fusion | flops 2020474880 | bytes 2887685 | tf_op jit(solution)/shard_map/while/body/eval_jaxpr/dot_general | solution.py:46
  86.5 0.7 slice.87
  87.4 0.1 fusion.34
  87.6 0.1 compare_select_fusion.3
  87.7 24.2 %reduce-scatter.2.cloned.1.call-done = f32[2,64,128]{2,1,0:T(8,128)} async-done(((f32[2,64,512]{2,1,0:T(8,128)}), f32[2,64,128]{2,1,0:T(8,128)}) %reduce-scatter.2.cloned.1.call-update) | async-done | bytes 65552 | tf_op jit(solution)/shard_map/reduce_scatter | solution.py:69
  111.9 0.9 slice_add_fusion
  112.8 0.1 pad_maximum_fusion.2
  112.9 1.1 copy.43
  114.0 5.1 %all-to-all-start = ((f32[2,64,8,256]{3,1,0,2:T(8,128)}), f32[2,64,8,256]{3,1,0,2:T(8,128)S(1)}, u32[]{:S(2)}, u32[]{:S(2)}) async-start(f32[2,64,8,256]{3,1,0,2:T(8,128)} %bitcast.38), calls=%async_computation.1 | async-start | bytes 2097152 | tf_op jit(solution)/shard_map/all_to_all | solution.py:77
  119.1 18.3 %select_multiply_fusion = f32[256,2,512]{2,1,0:T(2,128)S(1)} fusion(pred[256,2]{1,0:T(8,128)(4,1)S(1)} %fusion.34, f32[256,2]{1,0:T(8,128)S(1)} %compare_select_fusion.2, s32[256,2]{1,0:T(8,128)S(1)} %compare_select_fusion.3), kind=kLoop, calls=%fused_computation.40 | loop fusion | flops 4194304 | bytes 1053184 | tf_op jit(solution)/shard_map/mul | solution.py:25
  137.5 0.8 fusion.44
  138.3 0.9 pad_maximum_fusion.1
  139.3 1.8 stack.7
  141.2 4.3 %select_multiply_fusion.1 = f32[8,64,512]{2,1,0:T(8,128)S(1)} fusion(f32[8,64]{1,0:T(8,128)S(1)} %compare_select_fusion.6, s32[8,64]{1,0:T(8,128)S(1)} %compare_select_fusion.7, pred[8,64]{1,0:T(8,128)(4,1)S(1)} %fusion.40), kind=kLoop, calls=%fused_computation.41 | loop fusion | flops 4194304 | bytes 1053184 | tf_op jit(solution)/shard_map/mul | solution.py:25
  145.5 1.4 broadcast_multiply_fusion
  146.9 1.8 fusion.14
  148.8 17.9 %all_to_all.31 = f32[8,64,256]{2,1,0:T(8,128)S(1)} all-to-all(f32[8,64,256]{2,1,0:T(8,128)S(1)} %fusion.14), channel_id=1, replica_groups=mesh['dom'=4,'freq'=8] {'freq'}, dimensions={0} | all-to-all | bytes 1048576 | tf_op jit(solution)/shard_map/all_to_all | solution.py:82
  166.8 0.8 multiply_reduce_fusion
  167.5 0.3 reshape.233
  167.8 0.4 fusion.45
  168.4 4.3 %multiply_reduce_fusion.1 = (f32[]{:T(128)}, f32[32,2,2048]{2,1,0:T(2,128)S(1)}, f32[32,2,2048]{2,1,0:T(2,128)S(1)}) fusion(f32[32,2,2,2048]{3,2,1,0:T(2,128)S(1)} %copy-done.2, f32[32,2048]{1,0:T(8,128)S(1)} %bitcast.51, f32[32,2048]{1,0:T(8,128)S(1)} %bitcast.53), kind=kLoop, calls=%fused_computation.47 | loop fusion | flops 655359 | bytes 2621444 | tf_op jit(solution)/shard_map/reduce_sum | solution.py:88
  172.8 41.2 %all-reduce = (f32[]{:T(128)}, f32[]{:T(128)}) all-reduce(f32[]{:T(128)} %get-tuple-element.65, f32[]{:T(128)} %get-tuple-element.82), channel_id=1, replica_groups=mesh['dom'=4,'freq'=8] {'dom','freq'}, use_global_device_ids=true, to_apply=%region_4.5 | all-reduce | flops 2 | bytes 16 | tf_op jit(solution)/shard_map/psum | solution.py:87
  214.7 0.4 squeeze.23
  215.0 0.4 squeeze.24
  215.4 0.3 mul.219
  215.7 0.4 mul.220
  216.0 0.3 mul.223
  216.3 0.4 mul.224
  217.4 0.9 negate_multiply_fusion
  (45 shorter events, 0.9 us)
Async XLA Ops:
  7.2 104.8 %reduce-scatter.2.cloned.1.call-start = ((), (), s32[]{:S(2)}) async-start(), calls=%async_computation.3 | async-start | bytes 327680 | tf_op jit(solution)/shard_map/reduce_scatter | solution.py:69
  7.2 10.5 %copy-start.4 = (s32[2,4096]{1,0:T(2,128)S(1)}, s32[2,4096]{1,0:T(2,128)}, u32[]{:S(2)}) copy-start(s32[2,4096]{1,0:T(2,128)} %param.10) | copy-start | bytes 98308
  48.4 0.8 copy-start.5
  48.4 0.8 copy-start.6
  49.7 1.3 copy-start.1
  114.0 32.9 %all-to-all-start = ((f32[2,64,8,256]{3,1,0,2:T(8,128)}), f32[2,64,8,256]{3,1,0,2:T(8,128)S(1)}, u32[]{:S(2)}, u32[]{:S(2)}) async-start(f32[2,64,8,256]{3,1,0,2:T(8,128)} %bitcast.38), calls=%async_computation.1 | async-start | bytes 2097152 | tf_op jit(solution)/shard_map/all_to_all | solution.py:77
  146.9 19.8 %copy-start.3 = (f32[64,2048]{1,0:T(8,128)S(1)}, f32[64,2048]{1,0:T(8,128)}, u32[]{:S(2)}) copy-start(f32[64,2048]{1,0:T(8,128)} %param.9) | copy-start | bytes 1572868
  166.8 1.7 copy-start.2
  167.5 5.2 %copy-start = (f32[64,2048]{1,0:T(8,128)}, f32[64,2048]{1,0:T(8,128)S(1)}, u32[]{:S(2)}) copy-start(f32[64,2048]{1,0:T(8,128)S(1)} %get-tuple-element.83) | copy-start | bytes 1572868
Sparse Core Ops, SparseCore 0:
  87.4 24.4 reduce-scatter.1
where the time goes:
time: 227 us; the launch traced here: 226 us
  blocking collectives  68.1 us (30%)
  local copies, waits for them, and re-layouts  38.4 us (17%)
  matrix products  37 us (16%)
  other arithmetic  36.1 us (16%)
  waiting for transfers between devices  24.2 us (11%)
  between operations  17 us (7%)
  starting transfers between devices  5.19 us (2%)
    psum x1, blocking collectives, body(): lax.psum((jnp.sum(raw * raw), jnp.sum(residual * residual)), ('dom', 'fre...  41.2 us
    dot_general x8, matrix products, accumulate(): jnp.dot(flow_piece, signed, precision=lax.Precision.HIGHEST, preferred_el...  35.2 us
    gather x2, local copies, waits for them, and re-layouts, body(): across = extended[:, terminals[0]] - extended[:, terminals[1]]  28.2 us
    reduce_scatter x1, waiting for transfers between devices, body(): lax.psum_scatter(totals[:, :, node_count:], 'dom', scatter_dimension=2, t...  24.2 us
    mul x2, other arithmetic, transform_table(): forward = values * weight[:, None]  22.6 us
    all_to_all x1, blocking collectives, body(): lax.all_to_all(spectra, 'freq', split_axis=0, concat_axis=1, tiled=True)  17.9 us
    all_gather x1, blocking collectives, body(): lax.all_gather(voltages[:, :border_count], 'dom', axis=1, tiled=True)  8.96 us
    all_to_all x1, starting transfers between devices, body(): lax.all_to_all(grouped, 'freq', split_axis=2, concat_axis=1, tiled=True)  5.15 us
  transfers between devices with their start and end apart: 2, of which 1 were waited for; matrix products, arithmetic and copies ran while one was open for 12% of the time, Pallas kernels for 0%

commit v1 on v0

--- a/solution.py
+++ b/solution.py
@@ -85,7 +85,7 @@
     raw = -(jacobi[:, :, 0, :] * pairs[:, 0:1, :] + jacobi[:, :, 1, :] * pairs[:, 1:2, :])
     raw = raw.reshape(sample_rows, node_count)
     step_squares, residual_squares = lax.psum(
-        (jnp.sum(raw * raw), jnp.sum(residual * residual)), ("dom", "freq")
+        lax.psum((jnp.sum(raw * raw), jnp.sum(residual * residual)), "freq"), "dom"
     )
     entry_count = S * node_count * lax.axis_size("dom")
     spread = jnp.sqrt(step_squares / entry_count + 1e-06)

time: 227 us -> 214 us (0.943)
  the two profiles are of different devices: /device:TPU:12 before, /device:TPU:0 now
where the time goes in v1:
time: 214 us; the launch traced here: 213 us
  blocking collectives  55.4 us (26%)
  local copies, waits for them, and re-layouts  38.4 us (18%)
  matrix products  37 us (17%)
  other arithmetic  36.1 us (17%)
  waiting for transfers between devices  24.4 us (11%)
  between operations  17 us (8%)
  starting transfers between devices  4.64 us (2%)
    dot_general x8, matrix products, accumulate(): jnp.dot(flow_piece, signed, precision=lax.Precision.HIGHEST, preferred_el...  35.2 us
    gather x2, local copies, waits for them, and re-layouts, body(): across = extended[:, terminals[0]] - extended[:, terminals[1]]  28.2 us
    reduce_scatter x1, waiting for transfers between devices, body(): lax.psum_scatter(totals[:, :, node_count:], 'dom', scatter_dimension=2, t...  24.4 us
    mul x2, other arithmetic, transform_table(): forward = values * weight[:, None]  22.6 us
    all_to_all x1, blocking collectives, body(): lax.all_to_all(spectra, 'freq', split_axis=0, concat_axis=1, tiled=True)  20.2 us
    psum x1, blocking collectives, body(): lax.psum((jnp.sum(raw * raw), jnp.sum(residual * residual)), 'freq')  15.2 us
    all_gather x1, blocking collectives, body(): lax.all_gather(voltages[:, :border_count], 'dom', axis=1, tiled=True)  10.5 us
    psum x1, blocking collectives, body(): lax.psum(lax.psum((jnp.sum(raw * raw), jnp.sum(residual * residual)), 'fr...  9.54 us
  transfers between devices with their start and end apart: 2, of which 1 were waited for; matrix products, arithmetic and copies ran while one was open for 13% of the time, Pallas kernels for 0%

profile of v1, /device:TPU:0, one launch (start us, length us, event | category | flops | bytes accessed | tf_op | source)
XLA Modules:
  0.0 213.2 jit_solution(14607996227662126171)
XLA Ops:
  7.2 1.4 copy.26
  8.6 10.5 %all_gather.3 = f32[64,512]{0,1:T(8,128)S(1)} all-gather(f32[64,128]{0,1:T(8,128)S(1)} %slice.85), channel_id=1, replica_groups=mesh['dom'=4,'freq'=8] {'dom'}, dimensions={1}, use_global_device_ids=true | all-gather | bytes 163840 | tf_op jit(solution)/shard_map/all_gather | solution.py:60
  19.3 14.1 %gather_fusion = f32[4096,64]{1,0:T(8,128)} fusion(f32[64,2560]{0,1:T(8,128)S(1)} %pad_maximum_fusion, s32[4096]{0:T(1024)S(1)} %broadcast_clamp_fusion.1), kind=kCustom, calls=%fused_computation | custom fusion | bytes 2113536 | tf_op jit(solution)/shard_map/gather | solution.py:62
  33.4 14.1 %gather_fusion.1 = f32[4096,64]{1,0:T(8,128)} fusion(f32[64,2560]{0,1:T(8,128)S(1)} %pad_maximum_fusion, s32[4096]{0:T(1024)S(1)} %broadcast_clamp_fusion), kind=kCustom, calls=%fused_computation.1 | custom fusion | bytes 2113536 | tf_op jit(solution)/shard_map/gather | solution.py:62
  47.4 2.4 %sub.30 = f32[4096,64]{1,0:T(8,128)S(1)} subtract(f32[4096,64]{1,0:T(8,128)} %gather_fusion, f32[4096,64]{1,0:T(8,128)} %gather_fusion.1) | non-fusion elementwise | flops 262144 | bytes 3145728 | tf_op jit(solution)/shard_map/sub | solution.py:62
  49.9 0.6 copy.27
  50.5 0.1 copy-done.5
  50.7 0.2 slice_reduce_fusion.3
  50.9 0.3 multiply_add_fusion.1
  51.2 0.2 maximum_bitcast_fusion
  51.4 1.1 copy-done.1
  52.5 35.5 %while.12 = (s32[]{:T(128)}, f32[128,2560]{1,0:T(8,128)S(1)}, f32[8,128,512]{2,1,0:T(8,128)S(1)}, s32[8,2,512]{2,1,0:T(2,128)S(1)}, s32[]{:T(128)}, /*index=5*/s32[]{:T(128)}, s32[]{}) while((s32[]{:T(128)}, f32[128,2560]{1,0:T(8,128)S(1)}, f32[8,128,512]{2,1,0:T(8,128)S(1)}, s32[8,2,512]{2,1,0:T(2,128)S(1)}, ...), condition=%wide.region_1.2_spmd.clone.clone, body=%wide.region_0.1_spmd.clone.clone.sunk | while | flops 2020474880 | bytes 2895983 | solution.py:52
  52.5 4.4 %fusion.52 = f32[128,2560]{1,0:T(8,128)S(1)} fusion(s32[512]{0:T(512)S(1)} %bitcast.65, s32[512]{0:T(512)S(1)} %bitcast.64, f32[128,2560]{1,0:T(8,128)S(1)} %get-tuple-element.135, pred[]{:T(512)S(6)} %compare.14, f32[8,128,512]{2,1,0:T(8,128)S(1)} %get-tuple-element.143, s32[]{:T(128)} %get-tuple-element.134), kind=kOutput, calls=%fused_computation.9.clone.1 | convolution fusion | flops 2020474880 | bytes 2887685 | tf_op jit(solution)/shard_map/while/body/eval_jaxpr/dot_general | solution.py:46
  57.0 4.4 %fusion.52 = f32[128,2560]{1,0:T(8,128)S(1)} fusion(s32[512]{0:T(512)S(1)} %bitcast.65, s32[512]{0:T(512)S(1)} %bitcast.64, f32[128,2560]{1,0:T(8,128)S(1)} %get-tuple-element.135, pred[]{:T(512)S(6)} %compare.14, f32[8,128,512]{2,1,0:T(8,128)S(1)} %get-tuple-element.143, s32[]{:T(128)} %get-tuple-element.134), kind=kOutput, calls=%fused_computation.9.clone.1 | convolution fusion | flops 2020474880 | bytes 2887685 | tf_op jit(solution)/shard_map/while/body/eval_jaxpr/dot_general | solution.py:46
  61.4 4.4 %fusion.52 = f32[128,2560]{1,0:T(8,128)S(1)} fusion(s32[512]{0:T(512)S(1)} %bitcast.65, s32[512]{0:T(512)S(1)} %bitcast.64, f32[128,2560]{1,0:T(8,128)S(1)} %get-tuple-element.135, pred[]{:T(512)S(6)} %compare.14, f32[8,128,512]{2,1,0:T(8,128)S(1)} %get-tuple-element.143, s32[]{:T(128)} %get-tuple-element.134), kind=kOutput, calls=%fused_computation.9.clone.1 | convolution fusion | flops 2020474880 | bytes 2887685 | tf_op jit(solution)/shard_map/while/body/eval_jaxpr/dot_general | solution.py:46
  65.9 4.4 %fusion.52 = f32[128,2560]{1,0:T(8,128)S(1)} fusion(s32[512]{0:T(512)S(1)} %bitcast.65, s32[512]{0:T(512)S(1)} %bitcast.64, f32[128,2560]{1,0:T(8,128)S(1)} %get-tuple-element.135, pred[]{:T(512)S(6)} %compare.14, f32[8,128,512]{2,1,0:T(8,128)S(1)} %get-tuple-element.143, s32[]{:T(128)} %get-tuple-element.134), kind=kOutput, calls=%fused_computation.9.clone.1 | convolution fusion | flops 2020474880 | bytes 2887685 | tf_op jit(solution)/shard_map/while/body/eval_jaxpr/dot_general | solution.py:46
  70.3 4.4 %fusion.52 = f32[128,2560]{1,0:T(8,128)S(1)} fusion(s32[512]{0:T(512)S(1)} %bitcast.65, s32[512]{0:T(512)S(1)} %bitcast.64, f32[128,2560]{1,0:T(8,128)S(1)} %get-tuple-element.135, pred[]{:T(512)S(6)} %compare.14, f32[8,128,512]{2,1,0:T(8,128)S(1)} %get-tuple-element.143, s32[]{:T(128)} %get-tuple-element.134), kind=kOutput, calls=%fused_computation.9.clone.1 | convolution fusion | flops 2020474880 | bytes 2887685 | tf_op jit(solution)/shard_map/while/body/eval_jaxpr/dot_general | solution.py:46
  74.7 4.4 %fusion.52 = f32[128,2560]{1,0:T(8,128)S(1)} fusion(s32[512]{0:T(512)S(1)} %bitcast.65, s32[512]{0:T(512)S(1)} %bitcast.64, f32[128,2560]{1,0:T(8,128)S(1)} %get-tuple-element.135, pred[]{:T(512)S(6)} %compare.14, f32[8,128,512]{2,1,0:T(8,128)S(1)} %get-tuple-element.143, s32[]{:T(128)} %get-tuple-element.134), kind=kOutput, calls=%fused_computation.9.clone.1 | convolution fusion | flops 2020474880 | bytes 2887685 | tf_op jit(solution)/shard_map/while/body/eval_jaxpr/dot_general | solution.py:46
  79.2 4.4 %fusion.52 = f32[128,2560]{1,0:T(8,128)S(1)} fusion(s32[512]{0:T(512)S(1)} %bitcast.65, s32[512]{0:T(512)S(1)} %bitcast.64, f32[128,2560]{1,0:T(8,128)S(1)} %get-tuple-element.135, pred[]{:T(512)S(6)} %compare.14, f32[8,128,512]{2,1,0:T(8,128)S(1)} %get-tuple-element.143, s32[]{:T(128)} %get-tuple-element.134), kind=kOutput, calls=%fused_computation.9.clone.1 | convolution fusion | flops 2020474880 | bytes 2887685 | tf_op jit(solution)/shard_map/while/body/eval_jaxpr/dot_general | solution.py:46
  83.6 4.4 %fusion.52 = f32[128,2560]{1,0:T(8,128)S(1)} fusion(s32[512]{0:T(512)S(1)} %bitcast.65, s32[512]{0:T(512)S(1)} %bitcast.64, f32[128,2560]{1,0:T(8,128)S(1)} %get-tuple-element.135, pred[]{:T(512)S(6)} %compare.14, f32[8,128,512]{2,1,0:T(8,128)S(1)} %get-tuple-element.143, s32[]{:T(128)} %get-tuple-element.134), kind=kOutput, calls=%fused_computation.9.clone.1 | convolution fusion | flops 2020474880 | bytes 2887685 | tf_op jit(solution)/shard_map/while/body/eval_jaxpr/dot_general | solution.py:46
  88.0 0.7 slice.87
  88.9 0.1 fusion.34
  89.1 0.1 compare_select_fusion.3
  89.2 24.4 %reduce-scatter.2.cloned.1.call-done = f32[2,64,128]{2,1,0:T(8,128)} async-done(((f32[2,64,512]{2,1,0:T(8,128)}), f32[2,64,128]{2,1,0:T(8,128)}) %reduce-scatter.2.cloned.1.call-update) | async-done | bytes 65552 | tf_op jit(solution)/shard_map/reduce_scatter | solution.py:69
  113.6 0.9 slice_add_fusion
  114.5 1.1 copy.43
  115.6 4.6 %all-to-all-start = ((f32[2,64,8,256]{3,1,0,2:T(8,128)}), f32[2,64,8,256]{3,1,0,2:T(8,128)S(1)}, u32[]{:S(2)}, u32[]{:S(2)}) async-start(f32[2,64,8,256]{3,1,0,2:T(8,128)} %bitcast.38), calls=%async_computation.1 | async-start | bytes 2097152 | tf_op jit(solution)/shard_map/all_to_all | solution.py:77
  120.2 18.3 %select_multiply_fusion = f32[256,2,512]{2,1,0:T(2,128)S(1)} fusion(pred[256,2]{1,0:T(8,128)(4,1)S(1)} %fusion.34, f32[256,2]{1,0:T(8,128)S(1)} %compare_select_fusion.2, s32[256,2]{1,0:T(8,128)S(1)} %compare_select_fusion.3), kind=kLoop, calls=%fused_computation.40 | loop fusion | flops 4194304 | bytes 1053184 | tf_op jit(solution)/shard_map/mul | solution.py:25
  138.6 0.8 fusion.44
  139.4 0.9 pad_maximum_fusion.1
  140.3 1.8 stack.7
  142.3 4.3 %select_multiply_fusion.1 = f32[8,64,512]{2,1,0:T(8,128)S(1)} fusion(f32[8,64]{1,0:T(8,128)S(1)} %compare_select_fusion.6, s32[8,64]{1,0:T(8,128)S(1)} %compare_select_fusion.7, pred[8,64]{1,0:T(8,128)(4,1)S(1)} %fusion.40), kind=kLoop, calls=%fused_computation.41 | loop fusion | flops 4194304 | bytes 1053184 | tf_op jit(solution)/shard_map/mul | solution.py:25
  146.6 1.4 broadcast_multiply_fusion
  148.0 1.8 fusion.14
  149.9 20.2 %all_to_all.31 = f32[8,64,256]{2,1,0:T(8,128)S(1)} all-to-all(f32[8,64,256]{2,1,0:T(8,128)S(1)} %fusion.14), channel_id=1, replica_groups=mesh['dom'=4,'freq'=8] {'freq'}, dimensions={0} | all-to-all | bytes 1048576 | tf_op jit(solution)/shard_map/all_to_all | solution.py:82
  170.1 0.8 multiply_reduce_fusion
  170.9 0.3 reshape.233
  171.2 0.4 fusion.45
  171.8 4.3 %multiply_reduce_fusion.1 = (f32[]{:T(128)}, f32[32,2,2048]{2,1,0:T(2,128)S(1)}, f32[32,2,2048]{2,1,0:T(2,128)S(1)}) fusion(f32[32,2,2,2048]{3,2,1,0:T(2,128)S(1)} %copy-done.2, f32[32,2048]{1,0:T(8,128)S(1)} %bitcast.51, f32[32,2048]{1,0:T(8,128)S(1)} %bitcast.53), kind=kLoop, calls=%fused_computation.47 | loop fusion | flops 655359 | bytes 2621444 | tf_op jit(solution)/shard_map/reduce_sum | solution.py:88
  176.1 15.2 %all-reduce = (f32[]{:T(128)}, f32[]{:T(128)}) all-reduce(f32[]{:T(128)} %get-tuple-element.65, f32[]{:T(128)} %get-tuple-element.84), channel_id=1, replica_groups=mesh['dom'=4,'freq'=8] {'freq'}, use_global_device_ids=true, to_apply=%region_4.5 | all-reduce | flops 2 | bytes 16 | tf_op jit(solution)/shard_map/psum | solution.py:88
  191.3 9.5 %all-reduce.1 = (f32[]{:T(128)}, f32[]{:T(128)}) all-reduce(f32[]{:T(128)} %get-tuple-element.80, f32[]{:T(128)} %get-tuple-element.81), channel_id=1, replica_groups=mesh['dom'=4,'freq'=8] {'dom'}, use_global_device_ids=true, to_apply=%region_5.6 | all-reduce | flops 2 | bytes 16 | tf_op jit(solution)/shard_map/psum | solution.py:87
  201.5 0.4 squeeze.23
  201.9 0.4 squeeze.24
  202.3 0.3 mul.219
  202.6 0.4 mul.220
  202.9 0.3 mul.223
  203.2 0.4 mul.224
  204.3 0.9 negate_multiply_fusion
  (46 shorter events, 1.0 us)
Async XLA Ops:
  7.2 106.4 %reduce-scatter.2.cloned.1.call-start = ((), (), s32[]{:S(2)}) async-start(), calls=%async_computation.3 | async-start | bytes 327680 | tf_op jit(solution)/shard_map/reduce_scatter | solution.py:69
  7.2 12.0 %copy-start.4 = (s32[2,4096]{1,0:T(2,128)S(1)}, s32[2,4096]{1,0:T(2,128)}, u32[]{:S(2)}) copy-start(s32[2,4096]{1,0:T(2,128)} %param.10) | copy-start | bytes 98308
  49.9 0.8 copy-start.5
  49.9 0.8 copy-start.6
  51.2 1.3 copy-start.1
  115.6 32.3 %all-to-all-start = ((f32[2,64,8,256]{3,1,0,2:T(8,128)}), f32[2,64,8,256]{3,1,0,2:T(8,128)S(1)}, u32[]{:S(2)}, u32[]{:S(2)}) async-start(f32[2,64,8,256]{3,1,0,2:T(8,128)} %bitcast.38), calls=%async_computation.1 | async-start | bytes 2097152 | tf_op jit(solution)/shard_map/all_to_all | solution.py:77
  148.0 22.1 %copy-start.3 = (f32[64,2048]{1,0:T(8,128)S(1)}, f32[64,2048]{1,0:T(8,128)}, u32[]{:S(2)}) copy-start(f32[64,2048]{1,0:T(8,128)} %param.9) | copy-start | bytes 1572868
  170.1 1.7 copy-start.2
  170.9 5.2 %copy-start = (f32[64,2048]{1,0:T(8,128)}, f32[64,2048]{1,0:T(8,128)S(1)}, u32[]{:S(2)}) copy-start(f32[64,2048]{1,0:T(8,128)S(1)} %get-tuple-element.85) | copy-start | bytes 1572868
Sparse Core Ops, SparseCore 0:
  88.9 24.6 reduce-scatter.1
